TPU v7x, 256 devices: a whole 4x4x8 slice. The times are simulated.
256 devices in a mesh: qrow: 16 (over x_hi, y, core), dbcol: 16 (over z, x_lo).
Axes of the slice: x: 4 (x_hi: 2, x_lo: 2; x = x_hi * 2 + x_lo), y: 4, z: 8, core: 2. Of those that a mesh axis runs over, the one named last changes fastest.
Arguments:
- query_desc: bfloat16 [8192, 1024], P('qrow', 'dbcol'), may hold values from -0.1875 to 0.1875
- base_desc: bfloat16 [4096, 1024], P('dbcol', 'qrow'), may hold values from -6 to 6
- slopes: int32 [5], replicated, may hold values from -3 to 3, as said below
Outputs:
- seq_score: bfloat16 [8192, 4096], P('qrow', 'dbcol')
- best_score: float32 [8192], P('qrow')
Inputs may be any that keep to these rules, and one draw needn't show every extreme that they name: `slopes`: 5 distinct values that always include -3 and 3.
All inputs are finite; a program needn't handle non-finite values.
Results may differ from a plain program's by a relative error of at most 0.0041.
Values may be sent and summed in bfloat16 or wider, within the bound.
No kernel may reach another device: no remote copies, remote signals or barrier semaphores. Data moves between devices by JAX's collectives and lax.ppermute only.
A program may use at most 64 MiB of HBM per device.

v0:
```python
import math
import jax
import jax.numpy as jnp
from jax import lax
from jax.sharding import PartitionSpec as P

SEQ = 20
WIN = 10
NSLOPE = 5
ROWS_UP = 19
REACH = 57
HALO = 62
spread_floor = 0.5


def with_halo(cells, sides, width):
    for axis, dim in sides:
        count = lax.axis_size(axis)
        ends = count - 1
        head = lax.slice_in_dim(cells, 0, width, axis=dim)
        tail = lax.slice_in_dim(cells, cells.shape[dim] - width, cells.shape[dim], axis=dim)
        cells = jnp.concatenate(
            [
                lax.ppermute(tail, axis, [(i, (i + 1) % count) for i in range(ends)]),
                cells,
                lax.ppermute(head, axis, [((i + 1) % count, i) for i in range(ends)]),
            ],
            axis=dim,
        )
    return cells


def passed_along(x, axis, by):
    peers = lax.axis_size(axis)
    pairs = [(i, i + by) for i in range(peers) if 0 <= i + by < peers]
    return lax.ppermute(x, axis, pairs)


def normalize(similar, valid_cols, valid_rows, out_cols):
    half_win = WIN // 2
    weights = valid_cols.astype(jnp.float32)
    masked = similar * weights[None, :]
    window_sum = masked[:, 0:out_cols]
    window_sq = window_sum * window_sum
    counts = weights[0:out_cols]
    for offset in range(1, WIN):
        column = masked[:, offset : offset + out_cols]
        window_sum = window_sum + column
        window_sq = window_sq + column * column
        counts = counts + weights[offset : offset + out_cols]
    counts = jnp.maximum(counts, 1.0)[None, :]
    window_mean = window_sum / counts
    window_var = window_sq / counts - window_mean * window_mean
    spread = jnp.sqrt(jnp.maximum(window_var, 0.0))
    middle = similar[:, half_win : half_win + out_cols]
    normed = (middle - window_mean) / jnp.maximum(spread, spread_floor)
    keep = (
        weights[half_win : half_win + out_cols][None, :] * valid_rows.astype(jnp.float32)[:, None]
    )
    return (normed * keep).astype(jnp.bfloat16)


def sequence_scores(normed, slopes, tile_rows, tile_cols):
    best_sum = None
    for slope_pos in range(NSLOPE):
        slope_now = slopes[slope_pos]
        running = jnp.zeros((tile_rows, tile_cols), jnp.float32)
        for back_step in range(SEQ):
            row_first = jnp.int32(ROWS_UP - back_step)
            col_first = REACH - slope_now * back_step
            window = lax.dynamic_slice(normed, (row_first, col_first), (tile_rows, tile_cols))
            running = running + window.astype(jnp.float32)
        best_sum = running if best_sum is None else jnp.maximum(best_sum, running)
    return best_sum * (1.0 / math.sqrt(SEQ))


def local(query_desc, base_desc, slopes):
    tile_rows = query_desc.shape[0]
    tile_cols = base_desc.shape[0]
    col_index = lax.axis_index("dbcol")
    total_cols = tile_cols * lax.axis_size("dbcol")
    column_ids = col_index * tile_cols + jnp.arange(tile_cols + 2 * HALO, dtype=jnp.int32) - HALO
    valid_cols = (column_ids >= 0) & (column_ids < total_cols)
    query_full = lax.all_gather(query_desc, "dbcol", axis=1, tiled=True)
    base_full = lax.all_gather(base_desc, "qrow", axis=1, tiled=True)
    similar = lax.dot_general(
        query_full, base_full, (((1,), (1,)), ((), ())), preferred_element_type=jnp.float32
    )
    widened = with_halo(similar, (("dbcol", 1),), HALO)
    own_rows = jnp.ones((tile_rows,), jnp.bool_)
    normed_core = normalize(widened, valid_cols, own_rows, tile_cols + 2 * REACH)
    upper_normed = passed_along(normed_core[tile_rows - ROWS_UP :], "qrow", 1)
    normed = jnp.concatenate([upper_normed, normed_core], 0)
    scores = sequence_scores(normed, slopes, tile_rows, tile_cols)
    best_sum = lax.pmax(jnp.max(scores, axis=1), "dbcol")
    return (scores.astype(jnp.bfloat16), best_sum)


def solution(mesh):
    placed = (P("qrow", "dbcol"), P("dbcol", "qrow"), P())
    return jax.shard_map(
        local,
        mesh=mesh,
        in_specs=placed,
        out_specs=(P("qrow", "dbcol"), P("qrow")),
        check_vma=False,
    )
```

profile of v0, /device:TPU:4, one launch (start us, length us, event | category | flops | bytes accessed | tf_op | source)
XLA Modules:
  0.0 200.3 jit_solution(1408523695805401262)
XLA Ops:
  7.2 0.0 all-gather.2.cloned.1.call-start
  7.2 0.0 copy-start.1
  7.2 0.7 all-gather.2.cloned.1.call-update
  7.9 0.0 copy-done.1
  7.9 0.7 fusion.200
  73.0 0.0 copy-start
  73.1 0.7 copy-done
  73.8 23.3 %all_gather.7 = bf16[256,1024]{0,1:T(8,128)(2,1)S(1)} all-gather(bf16[256,64]{0,1:T(8,128)(2,1)S(1)} %copy-done), channel_id=1, replica_groups=mesh['qrow'=16,'dbcol'=16] {'qrow'}, dimensions={1}, use_global_device_ids=true | all-gather | bytes 557056 | tf_op jit(solution)/shard_map/all_gather | solution.py:85
  97.1 0.0 all-gather.2.cloned.1.call-done
  97.1 1.7 fusion.201
  98.9 4.0 %collective-permute-start = (f32[512,62]{0,1:T(8,128)S(1)}, f32[512,62]{0,1:T(8,128)S(1)}, u32[]{:S(2)}, u32[]{:S(2)}) collective-permute-start(f32[512,62]{0,1:T(8,128)S(1)} %get-tuple-element.8), channel_id=1, source_target_pairs={{0,1},{1,2},{2,3},{3,4},{4,5},{5,6},{6,7},{7,8},{8,9},{9,10},{10,1... | collective-permute-start | bytes 380936 | tf_op jit(solution)/shard_map/ppermute | solution.py:24
  102.8 1.3 collective-permute-start.1
  104.1 0.1 add_maximum_fusion
  104.2 1.9 collective-permute-done
  106.1 4.1 %collective-permute-done.1 = f32[512,62]{0,1:T(8,128)S(1)} collective-permute-done((f32[512,62]{0,1:T(8,128)S(1)}, f32[512,62]{0,1:T(8,128)S(1)}, u32[]{:S(2)}, u32[]{:S(2)}) %collective-permute-start.1) | collective-permute-done | bytes 127008 | tf_op jit(solution)/shard_map/ppermute | solution.py:26
  110.2 0.1 pad_maximum_fusion
  110.3 1.5 fusion.2
  111.8 0.1 slice.130
  111.9 2.1 %collective-permute-start.2 = (bf16[19,370]{0,1:T(8,128)(2,1)S(1)}, bf16[19,370]{0,1:T(8,128)(2,1)S(1)}, u32[]{:S(2)}, u32[]{:S(2)}) collective-permute-start(bf16[19,370]{0,1:T(8,128)(2,1)S(1)} %slice.130), channel_id=1, source_target_pairs={{0,16},{16,32},{32,48},{48,64},{64,80},{80,96},{96,112},{112,128},... | collective-permute-start | bytes 42188 | tf_op jit(solution)/shard_map/ppermute | solution.py:36
  114.8 6.7 %collective-permute-done.2 = bf16[19,370]{0,1:T(8,128)(2,1)S(1)} collective-permute-done((bf16[19,370]{0,1:T(8,128)(2,1)S(1)}, bf16[19,370]{0,1:T(8,128)(2,1)S(1)}, u32[]{:S(2)}, u32[]{:S(2)}) %collective-permute-start.2) | collective-permute-done | bytes 14092 | tf_op jit(solution)/shard_map/ppermute | solution.py:36
  121.5 35.1 %fusion.197 = (f32[512]{0:T(512)S(1)}, bf16[512,256]{0,1:T(8,128)(2,1)S(1)}) fusion(s32[]{:T(128)S(6)} %select_n.379, s32[]{:T(128)S(6)} %select_n.378, s32[]{:T(128)S(6)} %select_n.377, s32[]{:T(128)S(6)} %select_n.376, s32[]{:T(128)S(6)} %select_n.375, s32[]{:T(128)S(6)} %select_n.374, s32[]{:T(128)S(6)} %select_n.373, s32[]{:T(128)S(6)} %select_n.372, ...), kind=kLoop, calls=%fused_computation.326 | loop fusion | flops 63307264 | bytes 1007996 | tf_op jit(solution)/shard_map/reduce_max | solution.py:95
  156.6 0.8 copy.5
  157.4 36.1 %pmax.7 = f32[512]{0:T(512)} all-reduce(f32[512]{0:T(512)S(1)} %get-tuple-element.4), channel_id=1, replica_groups=mesh['qrow'=16,'dbcol'=16] {'dbcol'}, use_global_device_ids=true, to_apply=%region_1.0 | all-reduce | flops 512 | bytes 4096 | tf_op jit(solution)/shard_map/pmax | solution.py:95
  (2 shorter events, 0.0 us)
Async XLA Ops:
  7.2 90.0 %all-gather.2.cloned.1.call-start = ((), (), s32[]{:S(2)}) async-start(), calls=%async_computation | async-start | bytes 1114112 | tf_op jit(solution)/shard_map/all_gather | solution.py:84
  7.2 0.7 copy-start.1
  73.0 0.8 copy-start
  98.9 7.2 %collective-permute-start = (f32[512,62]{0,1:T(8,128)S(1)}, f32[512,62]{0,1:T(8,128)S(1)}, u32[]{:S(2)}, u32[]{:S(2)}) collective-permute-start(f32[512,62]{0,1:T(8,128)S(1)} %get-tuple-element.8), channel_id=1, source_target_pairs={{0,1},{1,2},{2,3},{3,4},{4,5},{5,6},{6,7},{7,8},{8,9},{9,10},{10,1... | collective-permute-start | bytes 380936 | tf_op jit(solution)/shard_map/ppermute | solution.py:24
  102.8 7.4 %collective-permute-start.1 = (f32[512,62]{0,1:T(8,128)S(1)}, f32[512,62]{0,1:T(8,128)S(1)}, u32[]{:S(2)}, u32[]{:S(2)}) collective-permute-start(f32[512,62]{0,1:T(8,128)S(1)} %get-tuple-element.9), channel_id=1, source_target_pairs={{1,0},{2,1},{3,2},{4,3},{5,4},{6,5},{7,6},{8,7},{9,8},{10,9},{11,1... | collective-permute-start | bytes 380936 | tf_op jit(solution)/shard_map/ppermute | solution.py:26
  111.9 9.5 %collective-permute-start.2 = (bf16[19,370]{0,1:T(8,128)(2,1)S(1)}, bf16[19,370]{0,1:T(8,128)(2,1)S(1)}, u32[]{:S(2)}, u32[]{:S(2)}) collective-permute-start(bf16[19,370]{0,1:T(8,128)(2,1)S(1)} %slice.130), channel_id=1, source_target_pairs={{0,16},{16,32},{32,48},{48,64},{64,80},{80,96},{96,112},{112,128},... | collective-permute-start | bytes 42188 | tf_op jit(solution)/shard_map/ppermute | solution.py:36
Sparse Core Ops, SparseCore 0:
  9.8 71.3 all-gather.1
where the time goes:
time: 202 us; the launch traced here: 200 us
  between operations  79.4 us (39%)
  blocking collectives  59.4 us (29%)
  other arithmetic  36.8 us (18%)
  waiting for transfers between devices  13.3 us (7%)
  starting transfers between devices  7.38 us (4%)
  local copies, waits for them, and re-layouts  2.29 us (1%)
    pmax x1, blocking collectives, local(): best_sum = lax.pmax(jnp.max(scores, axis=1), 'dbcol')  36.1 us
    reduce_max x1, other arithmetic, local(): best_sum = lax.pmax(jnp.max(scores, axis=1), 'dbcol')  35.1 us
    all_gather x1, blocking collectives, local(): base_full = lax.all_gather(base_desc, 'qrow', axis=1, tiled=True)  23.3 us
    ppermute x1, waiting for transfers between devices, passed_along(): return lax.ppermute(x, axis, pairs)  6.67 us
    ppermute x1, waiting for transfers between devices, with_halo(): lax.ppermute(head, axis, [((i + 1) % count, i) for i in range(ends)])  4.12 us
  transfers between devices with their start and end apart: 4, of which 3 were waited for; matrix products, arithmetic and copies ran while one was open for 0% of the time, Pallas kernels for 0%

commit v1 on v0

--- a/solution.py
+++ b/solution.py
@@ -11,6 +11,13 @@
 REACH = 57
 HALO = 62
 spread_floor = 0.5
+
+
+def swapped_in(x, mesh_axis, along):
+    size = lax.axis_size(mesh_axis)
+    blocks = jnp.stack([x for _ in range(size)])
+    blocks = lax.all_to_all(blocks, mesh_axis, split_axis=0, concat_axis=0)
+    return jnp.concatenate(blocks, axis=along)
 
 
 def with_halo(cells, sides, width):
@@ -82,7 +89,7 @@
     column_ids = col_index * tile_cols + jnp.arange(tile_cols + 2 * HALO, dtype=jnp.int32) - HALO
     valid_cols = (column_ids >= 0) & (column_ids < total_cols)
     query_full = lax.all_gather(query_desc, "dbcol", axis=1, tiled=True)
-    base_full = lax.all_gather(base_desc, "qrow", axis=1, tiled=True)
+    base_full = swapped_in(base_desc, "qrow", 1)
     similar = lax.dot_general(
         query_full, base_full, (((1,), (1,)), ((), ())), preferred_element_type=jnp.float32
     )

time: 202 us -> 186 us (0.921)
  blocking collectives: 59.4 us -> 36.5 us
  starting transfers between devices: 7.38 us -> 14.1 us
    all_gather x1 -> x0, blocking collectives: 23.3 us -> none  [local(): base_full = lax.all_gather(base_desc, 'qrow', axis=1, tiled=True)]
    all_to_all x0 -> x1, starting transfers between devices: none -> 7.58 us  [swapped_in(): blocks = lax.all_to_all(blocks, mesh_axis, split_axis=0, concat_axis=0)]
  transfers between devices with their start and end apart: 4 -> 5, of which waited for: 3 -> 3; matrix products, arithmetic and copies ran while one was open for 0% -> 1% of each run, Pallas kernels for 0% -> 0%
where the time goes in v1:
time: 186 us; the launch traced here: 185 us
  between operations  79.9 us (43%)
  other arithmetic  36.8 us (20%)
  blocking collectives  36.5 us (20%)
  starting transfers between devices  14.1 us (8%)
  waiting for transfers between devices  13.6 us (7%)
  local copies, waits for them, and re-layouts  2.51 us (1%)
    pmax x1, blocking collectives, local(): best_sum = lax.pmax(jnp.max(scores, axis=1), 'dbcol')  36.5 us
    reduce_max x1, other arithmetic, local(): best_sum = lax.pmax(jnp.max(scores, axis=1), 'dbcol')  35.1 us
    all_to_all x1, starting transfers between devices, swapped_in(): blocks = lax.all_to_all(blocks, mesh_axis, split_axis=0, concat_axis=0)  7.58 us
    ppermute x1, waiting for transfers between devices, passed_along(): return lax.ppermute(x, axis, pairs)  6.67 us
    ppermute x1, waiting for transfers between devices, with_halo(): lax.ppermute(head, axis, [((i + 1) % count, i) for i in range(ends)])  4.57 us
  transfers between devices with their start and end apart: 5, of which 3 were waited for; matrix products, arithmetic and copies ran while one was open for 1% of the time, Pallas kernels for 0%

profile of v1, /device:TPU:4, one launch (start us, length us, event | category | flops | bytes accessed | tf_op | source)
XLA Modules:
  0.0 185.1 jit_solution(6000841861323679485)
XLA Ops:
  7.2 0.0 copy-start
  7.2 0.0 all-gather.2.cloned.1.call-start
  7.2 0.7 all-gather.2.cloned.1.call-update
  7.9 0.0 copy-done
  7.9 0.9 stack.2
  8.8 0.0 copy-start.1
  8.8 7.6 %all-to-all-start = ((bf16[16,256,64]{1,2,0:T(8,128)(2,1)}), bf16[16,256,64]{1,2,0:T(8,128)(2,1)S(1)}, u32[]{:S(2)}, u32[]{:S(2)}) async-start(bf16[16,256,64]{1,2,0:T(8,128)(2,1)} %stack.2), calls=%async_computation | async-start | bytes 1048576 | tf_op jit(solution)/shard_map/all_to_all | solution.py:19
  16.4 0.0 copy-done.1
  16.4 0.7 fusion.200
  82.1 0.0 all-to-all-done
  82.1 0.0 all-gather.2.cloned.1.call-done
  82.1 1.7 fusion.201
  83.9 3.1 %collective-permute-start = (f32[512,62]{0,1:T(8,128)S(1)}, f32[512,62]{0,1:T(8,128)S(1)}, u32[]{:S(2)}, u32[]{:S(2)}) collective-permute-start(f32[512,62]{0,1:T(8,128)S(1)} %get-tuple-element.10), channel_id=1, source_target_pairs={{0,1},{1,2},{2,3},{3,4},{4,5},{5,6},{6,7},{7,8},{8,9},{9,10},{10,1... | collective-permute-start | bytes 380936 | tf_op jit(solution)/shard_map/ppermute | solution.py:31
  87.0 1.3 collective-permute-start.1
  88.3 0.1 add_maximum_fusion
  88.4 1.6 collective-permute-done
  90.0 4.6 %collective-permute-done.1 = f32[512,62]{0,1:T(8,128)S(1)} collective-permute-done((f32[512,62]{0,1:T(8,128)S(1)}, f32[512,62]{0,1:T(8,128)S(1)}, u32[]{:S(2)}, u32[]{:S(2)}) %collective-permute-start.1) | collective-permute-done | bytes 127008 | tf_op jit(solution)/shard_map/ppermute | solution.py:33
  94.5 0.1 pad_maximum_fusion
  94.7 1.5 fusion.2
  96.2 0.1 slice.130
  96.3 2.1 %collective-permute-start.2 = (bf16[19,370]{0,1:T(8,128)(2,1)S(1)}, bf16[19,370]{0,1:T(8,128)(2,1)S(1)}, u32[]{:S(2)}, u32[]{:S(2)}) collective-permute-start(bf16[19,370]{0,1:T(8,128)(2,1)S(1)} %slice.130), channel_id=1, source_target_pairs={{0,16},{16,32},{32,48},{48,64},{64,80},{80,96},{96,112},{112,128},... | collective-permute-start | bytes 42188 | tf_op jit(solution)/shard_map/ppermute | solution.py:43
  99.2 6.7 %collective-permute-done.2 = bf16[19,370]{0,1:T(8,128)(2,1)S(1)} collective-permute-done((bf16[19,370]{0,1:T(8,128)(2,1)S(1)}, bf16[19,370]{0,1:T(8,128)(2,1)S(1)}, u32[]{:S(2)}, u32[]{:S(2)}) %collective-permute-start.2) | collective-permute-done | bytes 14092 | tf_op jit(solution)/shard_map/ppermute | solution.py:43
  105.8 35.1 %fusion.197 = (f32[512]{0:T(512)S(1)}, bf16[512,256]{0,1:T(8,128)(2,1)S(1)}) fusion(s32[]{:T(128)S(6)} %select_n.379, s32[]{:T(128)S(6)} %select_n.378, s32[]{:T(128)S(6)} %select_n.377, s32[]{:T(128)S(6)} %select_n.376, s32[]{:T(128)S(6)} %select_n.375, s32[]{:T(128)S(6)} %select_n.374, s32[]{:T(128)S(6)} %select_n.373, s32[]{:T(128)S(6)} %select_n.372, ...), kind=kLoop, calls=%fused_computation.326 | loop fusion | flops 63307264 | bytes 1007996 | tf_op jit(solution)/shard_map/reduce_max | solution.py:102
  140.9 0.8 copy.7
  141.7 36.5 %pmax.7 = f32[512]{0:T(512)} all-reduce(f32[512]{0:T(512)S(1)} %get-tuple-element.6), channel_id=1, replica_groups=mesh['qrow'=16,'dbcol'=16] {'dbcol'}, use_global_device_ids=true, to_apply=%region_1.0 | all-reduce | flops 512 | bytes 4096 | tf_op jit(solution)/shard_map/pmax | solution.py:102
  (2 shorter events, 0.0 us)
Async XLA Ops:
  7.2 0.8 copy-start
  7.2 74.9 %all-gather.2.cloned.1.call-start = ((), (), s32[]{:S(2)}) async-start(), calls=%async_computation.1 | async-start | bytes 1114112 | tf_op jit(solution)/shard_map/all_gather | solution.py:91
  8.8 7.6 %copy-start.1 = (s32[5]{0:T(128)S(1)}, s32[5]{0:T(128)}, u32[]{:S(2)}) copy-start(s32[5]{0:T(128)} %param.5) | copy-start | bytes 64
  8.8 73.3 %all-to-all-start = ((bf16[16,256,64]{1,2,0:T(8,128)(2,1)}), bf16[16,256,64]{1,2,0:T(8,128)(2,1)S(1)}, u32[]{:S(2)}, u32[]{:S(2)}) async-start(bf16[16,256,64]{1,2,0:T(8,128)(2,1)} %stack.2), calls=%async_computation | async-start | bytes 1048576 | tf_op jit(solution)/shard_map/all_to_all | solution.py:19
  83.9 6.1 %collective-permute-start = (f32[512,62]{0,1:T(8,128)S(1)}, f32[512,62]{0,1:T(8,128)S(1)}, u32[]{:S(2)}, u32[]{:S(2)}) collective-permute-start(f32[512,62]{0,1:T(8,128)S(1)} %get-tuple-element.10), channel_id=1, source_target_pairs={{0,1},{1,2},{2,3},{3,4},{4,5},{5,6},{6,7},{7,8},{8,9},{9,10},{10,1... | collective-permute-start | bytes 380936 | tf_op jit(solution)/shard_map/ppermute | solution.py:31
  87.0 7.6 %collective-permute-start.1 = (f32[512,62]{0,1:T(8,128)S(1)}, f32[512,62]{0,1:T(8,128)S(1)}, u32[]{:S(2)}, u32[]{:S(2)}) collective-permute-start(f32[512,62]{0,1:T(8,128)S(1)} %get-tuple-element.11), channel_id=1, source_target_pairs={{1,0},{2,1},{3,2},{4,3},{5,4},{6,5},{7,6},{8,7},{9,8},{10,9},{11,1... | collective-permute-start | bytes 380936 | tf_op jit(solution)/shard_map/ppermute | solution.py:33
  96.3 9.5 %collective-permute-start.2 = (bf16[19,370]{0,1:T(8,128)(2,1)S(1)}, bf16[19,370]{0,1:T(8,128)(2,1)S(1)}, u32[]{:S(2)}, u32[]{:S(2)}) collective-permute-start(bf16[19,370]{0,1:T(8,128)(2,1)S(1)} %slice.130), channel_id=1, source_target_pairs={{0,16},{16,32},{32,48},{48,64},{64,80},{80,96},{96,112},{112,128},... | collective-permute-start | bytes 42188 | tf_op jit(solution)/shard_map/ppermute | solution.py:43
Sparse Core Ops, SparseCore 0:
  9.8 71.3 all-gather.1
